TPU v7x, 256 devices: a whole 4x4x8 slice. The times are simulated.
256 devices in a mesh: wide: 32 (over x, z), narrow: 8 (over y, core).
Axes of the slice: x: 4, y: 4, z: 8, core: 2. Of those that a mesh axis runs over, the one named last changes fastest.
Arguments:
- hidden_in: bfloat16 [16384, 1664], P(('wide', 'narrow')), may hold values from -3 to 3
- queries: bfloat16 [16, 1024, 1664], P('narrow', 'wide'), may hold values from -24 to 24
- keys: bfloat16 [16, 1024, 1664], P('narrow', 'wide'), may hold values from -24 to 24
- values: bfloat16 [16, 1024, 1664], P('narrow', 'wide'), may hold values from -12 to 12
- out_weight: bfloat16 [1664, 1664], P('narrow', 'wide'), may hold values from -0.25 to 0.25
- merge_weight: bfloat16 [4, 1664, 1664], P(None, 'narrow', 'wide'), may hold values from -0.125 to 0.125
- segment_ids: int32 [4096], P('wide'), may hold values from 0 to 15, never falling along the last dimension, each value on 1 to 2560 neighbouring positions
- owners: int32 [4096, 1], P('wide'), may hold values from 0 to 31; in each aligned block of 128 rows (0 to 127, 128 to 255, ...) at most 8 rows name the same one
Outputs:
- hidden_out: bfloat16 [16384, 1664], P(('wide', 'narrow'))
- delivered: bfloat16 [8192, 1664], P('wide', 'narrow')
Inputs may be any that keep to these rules, and one draw needn't show every extreme that they name: `segment_ids`: never falling along the tokens; the largest image or clip holds exactly 2560 merged tokens. `owners`: among the merged tokens of one index of wide, at most 8 share an owner, and exactly 8 do for some owner.
All inputs are finite; a program needn't handle non-finite values.
Results may differ from a plain program's by a relative error of at most 0.025.
Values may be sent and summed in bfloat16 or wider, within the bound.
A program may use at most 64 MiB of HBM per device.

v0:
```python
import math
import jax
import jax.numpy as jnp
from jax import lax
from jax.sharding import PartitionSpec as P

HEAD_DIM = 104
NEG = -1e30


def shards(hidden_in, queries, keys, values, out_weight, merge_weight, segment_ids, owners):
    heads_here, packed_rows, packed_width = queries.shape
    tok_rows = packed_rows * 16
    local_width = heads_here * HEAD_DIM
    scale = 1.0 / math.sqrt(HEAD_DIM)
    tok_seg = jnp.repeat(segment_ids, 4)
    seg_packed = tok_seg.reshape(1, packed_rows, 16)
    gathered_out, gathered_merge = (
        lax.all_gather(out_weight, "wide", axis=1, tiled=True),
        lax.all_gather(merge_weight, "wide", axis=2, tiled=True),
    )
    query_heads = queries.reshape(heads_here, tok_rows, HEAD_DIM)

    def key_block(carry, key_rows, value_rows, seg_rows):
        keep = tok_seg[:, None] == seg_rows[None, :]
        best, total, accum = carry
        key_heads = key_rows.reshape(heads_here, -1, HEAD_DIM)
        value_heads = value_rows.reshape(heads_here, -1, HEAD_DIM)
        scores = (
            jnp.einsum("hqd,hkd->hqk", query_heads, key_heads, preferred_element_type=jnp.float32)
            * scale
        )
        scores = jnp.where(keep[None], scores, NEG)
        new_best = jnp.maximum(best, jnp.max(scores, axis=-1))
        weights = jnp.where(keep[None], jnp.exp(scores - new_best[..., None]), 0.0)
        factor = jnp.exp(best - new_best)
        total = total * factor + jnp.sum(weights, axis=-1)
        accum = accum * factor[..., None] + jnp.einsum(
            "hqk,hkd->hqd",
            weights.astype(jnp.bfloat16),
            value_heads,
            preferred_element_type=jnp.float32,
        )
        return (new_best, total, accum)

    start_state = (
        jnp.full((heads_here, tok_rows), NEG, jnp.float32),
        jnp.zeros((heads_here, tok_rows), jnp.float32),
        jnp.zeros((heads_here, tok_rows, HEAD_DIM), jnp.float32),
    )
    carry = start_state
    key_rows = lax.all_gather(keys, "wide", axis=1, tiled=True)
    value_rows = lax.all_gather(values, "wide", axis=1, tiled=True)
    seg_rows = lax.all_gather(seg_packed, "wide", axis=1, tiled=True)
    count = key_rows.shape[1]
    blocks = count // 32
    stacked = (
        key_rows.reshape(heads_here, blocks, 32, packed_width).transpose(1, 0, 2, 3),
        value_rows.reshape(heads_here, blocks, 32, packed_width).transpose(1, 0, 2, 3),
        seg_rows.reshape(blocks, 512),
    )

    def step_block(state, item):
        return (key_block(state, item[0], item[1], item[2]), None)

    carry, unused = lax.scan(step_block, carry, stacked)
    best, total, accum = carry
    attn = (
        (accum / total[..., None])
        .transpose(1, 0, 2)
        .reshape(tok_rows, local_width)
        .astype(jnp.bfloat16)
    )
    partial_mix = jnp.dot(attn, gathered_out, preferred_element_type=jnp.float32)
    summed_mix = lax.psum_scatter(
        partial_mix.astype(jnp.bfloat16), "narrow", scatter_dimension=0, tiled=True
    ).astype(jnp.float32)
    hidden_out = (hidden_in.astype(jnp.float32) + summed_mix).astype(jnp.bfloat16)
    whole_rows = lax.all_gather(hidden_out, "narrow", axis=0, tiled=True)
    my_columns = lax.dynamic_slice_in_dim(
        whole_rows, lax.axis_index("narrow") * local_width, local_width, 1
    )
    merged_rows = tok_rows // 4
    grouped = my_columns.reshape(merged_rows, 4, local_width)
    partial_feat = jnp.einsum(
        "gjc,jco->go", grouped, gathered_merge, preferred_element_type=jnp.float32
    )
    feature = lax.psum_scatter(
        partial_feat.astype(jnp.bfloat16), "narrow", scatter_dimension=1, tiled=True
    )
    owner_count = lax.axis_size("wide")
    capacity = 2 * merged_rows // owner_count
    owner_col = owners[:, 0]
    onehot = (owner_col[:, None] == jnp.arange(owner_count, dtype=jnp.int32)[None, :]).astype(
        jnp.int32
    )
    rank = jnp.sum(jnp.cumsum(onehot, axis=0) * onehot, axis=1) - 1
    slot = owner_col * capacity + rank
    picker = (jnp.arange(owner_count * capacity, dtype=jnp.int32)[:, None] == slot[None, :]).astype(
        jnp.bfloat16
    )
    outgoing = jnp.dot(picker, feature, preferred_element_type=jnp.float32).astype(jnp.bfloat16)
    outgoing = outgoing.reshape(owner_count, capacity, feature.shape[1])
    arrived = lax.all_to_all(outgoing, "wide", split_axis=0, concat_axis=0, tiled=True)
    return (hidden_out, arrived.reshape(owner_count * capacity, feature.shape[1]))


def solution(mesh):
    return jax.shard_map(
        shards,
        mesh=mesh,
        in_specs=(
            P(("wide", "narrow"), None),
            P("narrow", "wide", None),
            P("narrow", "wide", None),
            P("narrow", "wide", None),
            P("narrow", "wide"),
            P(None, "narrow", "wide"),
            P("wide"),
            P("wide", None),
        ),
        out_specs=(P(("wide", "narrow"), None), P("wide", "narrow")),
        check_vma=False,
    )
```

profile of v0, /device:TPU:32, one launch (start us, length us, event | category | flops | bytes accessed | tf_op | source)
XLA Modules:
  0.0 576.4 jit_solution(16896971549550113275)
XLA Ops:
  9.7 51.9 %all_gather.18 = s32[1,1024,16]{2,0,1:T(1,128)S(1)} all-gather(s32[1,32,16]{2,0,1:T(1,128)S(1)} %copy.25), channel_id=1, replica_groups=mesh['wide'=32,'narrow'=8] {'wide'}, dimensions={1}, use_global_device_ids=true | all-gather | bytes 67584 | tf_op jit(solution)/shard_map/all_gather | solution.py:54
  62.1 2.0 reduce.3
  65.1 49.1 %all-gather = bf16[32,52,208]{2,1,0:T(8,128)(2,1)S(1)} all-gather(bf16[1,52,208]{2,1,0:T(8,128)(2,1)S(1)} %bitcast.77), channel_id=1, replica_groups=mesh['wide'=32,'narrow'=8] {'wide'}, dimensions={0}, use_global_device_ids=true | all-gather | bytes 713856 | tf_op jit(solution)/shard_map/all_gather | solution.py:19
  114.2 1.3 reshape.93
  115.5 82.9 %all-gather.8.cloned.1.call-done = bf16[2,1024,1664]{2,1,0:T(8,128)(2,1)} async-done(((bf16[2,32,1664]{2,1,0:T(8,128)(2,1)}), bf16[2,1024,1664]{2,1,0:T(8,128)(2,1)}) %all-gather.8.cloned.1.call-update) | async-done | bytes 6815760 | tf_op jit(solution)/shard_map/all_gather | solution.py:53
  198.4 167.4 %while.15 = (s32[]{:T(128)}, f32[2,512]{1,0:T(2,128)S(1)}, f32[2,512]{1,0:T(2,128)S(1)}, f32[2,512,104]{1,2,0:T(8,128)S(1)}, s32[32,512]{1,0:T(8,128)S(1)}, /*in...) while((s32[]{:T(128)}, f32[2,512]{1,0:T(2,128)S(1)}, ...), condition=%wide.region_3.4_spmd.clone, body=%wide.region_0.3_spmd.clone.sunk | while | flops 225506304 | bytes 10615425 | solution.py:66
  199.5 1.1 dynamic-slice_bitcast_fusion.3
  204.7 1.1 dynamic-slice_bitcast_fusion.3
  209.9 1.1 dynamic-slice_bitcast_fusion.3
  215.2 1.1 dynamic-slice_bitcast_fusion.3
  220.4 1.1 dynamic-slice_bitcast_fusion.3
  225.6 1.1 dynamic-slice_bitcast_fusion.3
  230.9 1.1 dynamic-slice_bitcast_fusion.3
  236.1 1.1 dynamic-slice_bitcast_fusion.3
  241.3 1.1 dynamic-slice_bitcast_fusion.3
  246.6 1.1 dynamic-slice_bitcast_fusion.3
  251.8 1.1 dynamic-slice_bitcast_fusion.3
  257.0 1.1 dynamic-slice_bitcast_fusion.3
  262.3 1.1 dynamic-slice_bitcast_fusion.3
  267.5 1.1 dynamic-slice_bitcast_fusion.3
  272.7 1.1 dynamic-slice_bitcast_fusion.3
  278.0 1.1 dynamic-slice_bitcast_fusion.3
  283.2 1.1 dynamic-slice_bitcast_fusion.3
  288.4 1.1 dynamic-slice_bitcast_fusion.3
  293.7 1.1 dynamic-slice_bitcast_fusion.3
  298.9 1.1 dynamic-slice_bitcast_fusion.3
  304.1 1.1 dynamic-slice_bitcast_fusion.3
  309.4 1.1 dynamic-slice_bitcast_fusion.3
  314.6 1.1 dynamic-slice_bitcast_fusion.3
  319.8 1.1 dynamic-slice_bitcast_fusion.3
  325.1 1.1 dynamic-slice_bitcast_fusion.3
  330.3 1.1 dynamic-slice_bitcast_fusion.3
  335.5 1.1 dynamic-slice_bitcast_fusion.3
  340.7 1.1 dynamic-slice_bitcast_fusion.3
  346.0 1.1 dynamic-slice_bitcast_fusion.3
  351.2 1.1 dynamic-slice_bitcast_fusion.3
  356.4 1.1 dynamic-slice_bitcast_fusion.3
  361.7 1.1 dynamic-slice_bitcast_fusion.3
  365.9 3.1 convolution_convert_fusion
  369.0 33.3 %reduce-scatter.5.cloned.1.call-done = bf16[64,1664]{1,0:T(8,128)(2,1)} async-done(((bf16[512,1664]{1,0:T(8,128)(2,1)}), bf16[64,1664]{1,0:T(8,128)(2,1)}) %reduce-scatter.5.cloned.1.call-update) | async-done | bytes 213008 | tf_op jit(solution)/shard_map/reduce_scatter | solution.py:75
  402.4 1.7 add_convert_fusion
  404.7 26.0 %all-gather.10.cloned.1.call-done = bf16[512,1664]{1,0:T(8,128)(2,1)} async-done(((bf16[64,1664]{1,0:T(8,128)(2,1)}), bf16[512,1664]{1,0:T(8,128)(2,1)}) %all-gather.10.cloned.1.call-update) | async-done | bytes 1703952 | tf_op jit(solution)/shard_map/all_gather | solution.py:79
  430.8 1.1 constant_dynamic-slice_fusion.1
  432.0 81.6 %all-gather.12.cloned.1.call-done = bf16[4,208,1664]{1,0,2:T(4,128)(2,1)} async-done(((bf16[4,208,52]{1,0,2:T(4,128)(2,1)}), bf16[4,208,1664]{1,0,2:T(4,128)(2,1)}) %all-gather.12.cloned.1.call-update) | async-done | bytes 2768912 | tf_op jit(solution)/shard_map/all_gather | solution.py:20
  513.6 3.8 fusion.23
  517.9 30.2 %reduce-scatter.7.cloned.1.call-done = bf16[208,128]{1,0:T(8,128)(2,1)} async-done(((bf16[1664,128]{1,0:T(8,128)(2,1)}), bf16[208,128]{1,0:T(8,128)(2,1)}) %reduce-scatter.7.cloned.1.call-update) | async-done | bytes 53264
  548.1 1.0 convolution_convert_fusion.1
  549.2 19.6 %all_to_all.5 = bf16[32,8,208]{2,1,0:T(8,128)(2,1)S(1)} all-to-all(bf16[32,8,208]{2,1,0:T(8,128)(2,1)S(1)} %bitcast.71), channel_id=1, replica_groups=mesh['wide'=32,'narrow'=8] {'wide'}, dimensions={0} | all-to-all | bytes 212992 | tf_op jit(solution)/shard_map/all_to_all | solution.py:104
  (424 shorter events, 136.0 us)
Async XLA Ops:
  7.2 57.2 %copy-start.1 = (bf16[2,32,1664]{2,1,0:T(8,128)(2,1)S(1)}, bf16[2,32,1664]{2,1,0:T(8,128)(2,1)}, u32[]{:S(2)}) copy-start(bf16[2,32,1664]{2,1,0:T(8,128)(2,1)} %param.11) | copy-start | bytes 638980
  7.2 57.9 %copy-start.2 = (bf16[208,52]{0,1:T(8,128)(2,1)S(1)}, bf16[208,52]{0,1:T(8,128)(2,1)}, u32[]{:S(2)}) copy-start(bf16[208,52]{0,1:T(8,128)(2,1)} %param.14) | copy-start | bytes 64900
  7.2 108.3 %all-gather.6.cloned.1.call-start = ((), (), s32[]{:S(2)}) async-start(), calls=%async_computation.3 | async-start | bytes 7028736 | tf_op jit(solution)/shard_map/all_gather | solution.py:52
  7.9 190.5 %all-gather.8.cloned.1.call-start = ((), (), s32[]{:S(2)}) async-start(), calls=%async_computation.4 | async-start | bytes 7028736 | tf_op jit(solution)/shard_map/all_gather | solution.py:53
  8.7 393.7 %reduce-scatter.5.cloned.1.call-start = ((), (), s32[]{:S(2)}) async-start(), calls=%async_computation.5 | async-start | bytes 1916928 | tf_op jit(solution)/shard_map/reduce_scatter | solution.py:75
  365.9 36.5 %copy-start = (bf16[64,1664]{1,0:T(8,128)(2,1)S(1)}, bf16[64,1664]{1,0:T(8,128)(2,1)}, u32[]{:S(2)}) copy-start(bf16[64,1664]{1,0:T(8,128)(2,1)} %param.10) | copy-start | bytes 638980
  369.0 61.8 %all-gather.10.cloned.1.call-start = ((), (), s32[]{:S(2)}) async-start(), calls=%async_computation.6 | async-start | bytes 1916928 | tf_op jit(solution)/shard_map/all_gather | solution.py:79
  404.1 109.6 %all-gather.12.cloned.1.call-start = ((), (), s32[]{:S(2)}) async-start(), calls=%async_computation.7 | async-start | bytes 3514368 | tf_op jit(solution)/shard_map/all_gather | solution.py:20
  404.7 143.5 %reduce-scatter.7.cloned.1.call-start = ((), (), s32[]{:S(2)}) async-start(), calls=%async_computation.8 | async-start | bytes 479232
  432.0 85.4 %copy-start.3 = (s32[128,1]{0,1:T(1,128)S(1)}, s32[128,1]{0,1:T(1,128)}, u32[]{:S(2)}) copy-start(s32[128,1]{0,1:T(1,128)} %param.17) | copy-start | bytes 1540
Sparse Core Ops, SparseCore 0:
  10.6 96.3 all-gather.5
  109.6 88.7 all-gather.7
  369.1 33.2 reduce-scatter.4
  404.8 25.9 all-gather.9
  433.5 80.0 all-gather.11
  517.5 30.5 reduce-scatter.6
where the time goes:
time: 578 us; the launch traced here: 576 us
  waiting for transfers between devices  256 us (44%)
  blocking collectives  121 us (21%)
  local copies, waits for them, and re-layouts  101 us (17%)
  matrix products  50.9 us (9%)
  other arithmetic  30.1 us (5%)
  between operations  14.3 us (2%)
    all_gather x1, waiting for transfers between devices, shards(): value_rows = lax.all_gather(values, 'wide', axis=1, tiled=True)  82.9 us
    all_gather x1, waiting for transfers between devices, shards(): lax.all_gather(merge_weight, 'wide', axis=2, tiled=True)  81.6 us
    all_gather x1, blocking collectives, shards(): seg_rows = lax.all_gather(seg_packed, 'wide', axis=1, tiled=True)  51.9 us
    all_gather x1, blocking collectives, shards(): lax.all_gather(out_weight, 'wide', axis=1, tiled=True)  49.1 us
    dynamic_slice x64, local copies, waits for them, and re-layouts, shards(): carry, unused = lax.scan(step_block, carry, stacked)  34.9 us
    reduce_scatter x1, waiting for transfers between devices, shards(): lax.psum_scatter(partial_mix.astype(jnp.bfloat16), 'narrow', scatter_dime...  33.3 us
    unnamed x7, waiting for transfers between devices  32.2 us
    all_gather x1, waiting for transfers between devices, shards(): whole_rows = lax.all_gather(hidden_out, 'narrow', axis=0, tiled=True)  26 us
  transfers between devices with their start and end apart: 6, of which 5 were waited for; matrix products, arithmetic and copies ran while one was open for 1% of the time, Pallas kernels for 0%

commit v1 on v0

--- a/solution.py
+++ b/solution.py
@@ -15,9 +15,18 @@
     scale = 1.0 / math.sqrt(HEAD_DIM)
     tok_seg = jnp.repeat(segment_ids, 4)
     seg_packed = tok_seg.reshape(1, packed_rows, 16)
+    hold_table_here = lambda array_in: jnp.concatenate(
+        lax.all_to_all(
+            jnp.stack([array_in] * lax.axis_size("wide"), axis=0),
+            axis_name="wide",
+            split_axis=0,
+            concat_axis=0,
+        ),
+        axis=2,
+    )
     gathered_out, gathered_merge = (
         lax.all_gather(out_weight, "wide", axis=1, tiled=True),
-        lax.all_gather(merge_weight, "wide", axis=2, tiled=True),
+        hold_table_here(merge_weight),
     )
     query_heads = queries.reshape(heads_here, tok_rows, HEAD_DIM)
 

time: 578 us -> 521 us (0.901)
  waiting for transfers between devices: 256 us -> 189 us
  starting transfers between devices: 0.24 us -> 6.69 us
    all_gather x1 -> x0, waiting for transfers between devices: 81.6 us -> none  [shards(): lax.all_gather(merge_weight, 'wide', axis=2, tiled=True)]
    all_to_all x0 -> x1, waiting for transfers between devices: none -> 18.5 us  [shards(): lax.all_to_all(jnp.stack([array_in] * lax.axis_size('wide'), axis=0), axi...]
    reduce_scatter x1, waiting for transfers between devices: 33.3 us -> 24.7 us  [shards(): lax.psum_scatter(partial_mix.astype(jnp.bfloat16), 'narrow', scatter_dime...]
    all_to_all x0 -> x1, starting transfers between devices: none -> 6.49 us  [shards(): lax.all_to_all(jnp.stack([array_in] * lax.axis_size('wide'), axis=0), axi...]
    unnamed x7 -> x6, waiting for transfers between devices: 32.2 us -> 35.8 us
  transfers between devices with their start and end apart: 6 -> 6, of which waited for: 5 -> 5; matrix products, arithmetic and copies ran while one was open for 1% -> 3% of each run, Pallas kernels for 0% -> 0%
where the time goes in v1:
time: 521 us; the launch traced here: 519 us
  waiting for transfers between devices  189 us (36%)
  blocking collectives  121 us (23%)
  local copies, waits for them, and re-layouts  106 us (20%)
  matrix products  49.8 us (10%)
  other arithmetic  30.2 us (6%)
  between operations  13.9 us (3%)
  starting transfers between devices  6.69 us (1%)
    all_gather x1, waiting for transfers between devices, shards(): value_rows = lax.all_gather(values, 'wide', axis=1, tiled=True)  82.9 us
    all_gather x1, blocking collectives, shards(): seg_rows = lax.all_gather(seg_packed, 'wide', axis=1, tiled=True)  51.9 us
    all_gather x1, blocking collectives, shards(): lax.all_gather(out_weight, 'wide', axis=1, tiled=True)  49.1 us
    unnamed x6, waiting for transfers between devices  35.8 us
    dynamic_slice x64, local copies, waits for them, and re-layouts, shards(): carry, unused = lax.scan(step_block, carry, stacked)  34.9 us
    all_gather x1, waiting for transfers between devices, shards(): whole_rows = lax.all_gather(hidden_out, 'narrow', axis=0, tiled=True)  26.8 us
    dot_general x32, matrix products, key_block(): jnp.einsum('hqk,hkd->hqd', weights.astype(jnp.bfloat16), value_heads, pre...  25.8 us
    reduce_scatter x1, waiting for transfers between devices, shards(): lax.psum_scatter(partial_mix.astype(jnp.bfloat16), 'narrow', scatter_dime...  24.7 us
  transfers between devices with their start and end apart: 6, of which 5 were waited for; matrix products, arithmetic and copies ran while one was open for 3% of the time, Pallas kernels for 0%

profile of v1, /device:TPU:32, one launch (start us, length us, event | category | flops | bytes accessed | tf_op | source)
XLA Modules:
  0.0 519.1 jit_solution(10401100013935456285)
XLA Ops:
  9.7 51.9 %all_gather.15 = s32[1,1024,16]{2,0,1:T(1,128)S(1)} all-gather(s32[1,32,16]{2,0,1:T(1,128)S(1)} %copy.26), channel_id=1, replica_groups=mesh['wide'=32,'narrow'=8] {'wide'}, dimensions={1}, use_global_device_ids=true | all-gather | bytes 67584 | tf_op jit(solution)/shard_map/all_gather | solution.py:63
  62.1 2.0 reduce.3
  65.1 49.1 %all-gather = bf16[32,52,208]{2,1,0:T(8,128)(2,1)S(1)} all-gather(bf16[1,52,208]{2,1,0:T(8,128)(2,1)S(1)} %bitcast.81), channel_id=1, replica_groups=mesh['wide'=32,'narrow'=8] {'wide'}, dimensions={0}, use_global_device_ids=true | all-gather | bytes 713856 | tf_op jit(solution)/shard_map/all_gather | solution.py:28
  114.2 1.3 reshape.103
  115.5 82.9 %all-gather.7.cloned.1.call-done = bf16[2,1024,1664]{2,1,0:T(8,128)(2,1)} async-done(((bf16[2,32,1664]{2,1,0:T(8,128)(2,1)}), bf16[2,1024,1664]{2,1,0:T(8,128)(2,1)}) %all-gather.7.cloned.1.call-update) | async-done | bytes 6815760 | tf_op jit(solution)/shard_map/all_gather | solution.py:62
  198.4 167.3 %while.15 = (s32[]{:T(128)}, f32[2,512]{1,0:T(2,128)S(1)}, f32[2,512]{1,0:T(2,128)S(1)}, f32[2,512,104]{1,2,0:T(8,128)S(1)}, s32[32,512]{1,0:T(8,128)S(1)}, /*in...) while((s32[]{:T(128)}, f32[2,512]{1,0:T(2,128)S(1)}, ...), condition=%wide.region_3.4_spmd.clone, body=%wide.region_0.3_spmd.clone.sunk | while | flops 225506304 | bytes 10615425 | solution.py:75
  199.5 1.1 dynamic-slice_bitcast_fusion.3
  204.7 1.1 dynamic-slice_bitcast_fusion.3
  209.9 1.1 dynamic-slice_bitcast_fusion.3
  215.1 1.1 dynamic-slice_bitcast_fusion.3
  220.4 1.1 dynamic-slice_bitcast_fusion.3
  225.6 1.1 dynamic-slice_bitcast_fusion.3
  230.8 1.1 dynamic-slice_bitcast_fusion.3
  236.1 1.1 dynamic-slice_bitcast_fusion.3
  241.3 1.1 dynamic-slice_bitcast_fusion.3
  246.5 1.1 dynamic-slice_bitcast_fusion.3
  251.8 1.1 dynamic-slice_bitcast_fusion.3
  257.0 1.1 dynamic-slice_bitcast_fusion.3
  262.2 1.1 dynamic-slice_bitcast_fusion.3
  267.4 1.1 dynamic-slice_bitcast_fusion.3
  272.7 1.1 dynamic-slice_bitcast_fusion.3
  277.9 1.1 dynamic-slice_bitcast_fusion.3
  283.1 1.1 dynamic-slice_bitcast_fusion.3
  288.4 1.1 dynamic-slice_bitcast_fusion.3
  293.6 1.1 dynamic-slice_bitcast_fusion.3
  298.8 1.1 dynamic-slice_bitcast_fusion.3
  304.1 1.1 dynamic-slice_bitcast_fusion.3
  309.3 1.1 dynamic-slice_bitcast_fusion.3
  314.5 1.1 dynamic-slice_bitcast_fusion.3
  319.7 1.1 dynamic-slice_bitcast_fusion.3
  325.0 1.1 dynamic-slice_bitcast_fusion.3
  330.2 1.1 dynamic-slice_bitcast_fusion.3
  335.4 1.1 dynamic-slice_bitcast_fusion.3
  340.7 1.1 dynamic-slice_bitcast_fusion.3
  345.9 1.1 dynamic-slice_bitcast_fusion.3
  351.1 1.1 dynamic-slice_bitcast_fusion.3
  365.8 3.1 convolution_convert_fusion
  368.9 2.6 stack.2
  371.5 6.5 %all-to-all-start = ((bf16[32,4,208,52]{2,1,3,0:T(4,128)(2,1)}), bf16[32,4,208,52]{2,1,3,0:T(4,128)(2,1)S(1)}, u32[]{:S(2)}, u32[]{:S(2)}) async-start(bf16[32,4,208,52]{2,1,3,0:T(4,128)(2,1)} %stack.2), calls=%async_computation.1 | async-start | bytes 6815744 | tf_op jit(solution)/shard_map/all_to_all | solution.py:19
  378.1 24.7 %reduce-scatter.5.cloned.1.call-done = bf16[64,1664]{1,0:T(8,128)(2,1)} async-done(((bf16[512,1664]{1,0:T(8,128)(2,1)}), bf16[64,1664]{1,0:T(8,128)(2,1)}) %reduce-scatter.5.cloned.1.call-update) | async-done | bytes 213008 | tf_op jit(solution)/shard_map/reduce_scatter | solution.py:84
  402.8 1.8 add_convert_fusion
  404.7 26.8 %all-gather.9.cloned.1.call-done = bf16[512,1664]{1,0:T(8,128)(2,1)} async-done(((bf16[64,1664]{1,0:T(8,128)(2,1)}), bf16[512,1664]{1,0:T(8,128)(2,1)}) %all-gather.9.cloned.1.call-update) | async-done | bytes 1703952 | tf_op jit(solution)/shard_map/all_gather | solution.py:88
  431.5 1.8 constant_dynamic-slice_fusion.1
  433.3 1.7 reshape.97
  435.1 18.5 %all-to-all-done = bf16[32,4,208,52]{2,1,3,0:T(4,128)(2,1)S(1)} async-done(((bf16[32,4,208,52]{2,1,3,0:T(4,128)(2,1)}), bf16[32,4,208,52]{2,1,3,0:T(4,128)(2,1)S(1)}, u32[]{:S(2)}, u32[]{:S(2)}) %all-to-all-start) | async-done | bytes 2768928 | tf_op jit(solution)/shard_map/all_to_all | solution.py:19
  453.6 2.8 fusion.23
  456.8 34.4 %reduce-scatter.7.cloned.1.call-done = bf16[208,128]{1,0:T(8,128)(2,1)} async-done(((bf16[1664,128]{1,0:T(8,128)(2,1)}), bf16[208,128]{1,0:T(8,128)(2,1)}) %reduce-scatter.7.cloned.1.call-update) | async-done | bytes 53264
  492.3 19.5 %all_to_all.10 = bf16[32,8,208]{2,1,0:T(8,128)(2,1)S(1)} all-to-all(bf16[32,8,208]{2,1,0:T(8,128)(2,1)S(1)} %bitcast.75), channel_id=1, replica_groups=mesh['wide'=32,'narrow'=8] {'wide'}, dimensions={0} | all-to-all | bytes 212992 | tf_op jit(solution)/shard_map/all_to_all | solution.py:113
  (424 shorter events, 138.4 us)
Async XLA Ops:
  7.2 57.2 %copy-start = (bf16[2,32,1664]{2,1,0:T(8,128)(2,1)S(1)}, bf16[2,32,1664]{2,1,0:T(8,128)(2,1)}, u32[]{:S(2)}) copy-start(bf16[2,32,1664]{2,1,0:T(8,128)(2,1)} %param.11) | copy-start | bytes 638980
  7.2 57.9 %copy-start.2 = (bf16[208,52]{0,1:T(8,128)(2,1)S(1)}, bf16[208,52]{0,1:T(8,128)(2,1)}, u32[]{:S(2)}) copy-start(bf16[208,52]{0,1:T(8,128)(2,1)} %param.14) | copy-start | bytes 64900
  7.2 108.3 %all-gather.5.cloned.1.call-start = ((), (), s32[]{:S(2)}) async-start(), calls=%async_computation.4 | async-start | bytes 7028736 | tf_op jit(solution)/shard_map/all_gather | solution.py:61
  7.9 190.5 %all-gather.7.cloned.1.call-start = ((), (), s32[]{:S(2)}) async-start(), calls=%async_computation.5 | async-start | bytes 7028736 | tf_op jit(solution)/shard_map/all_gather | solution.py:62
  8.7 394.1 %reduce-scatter.5.cloned.1.call-start = ((), (), s32[]{:S(2)}) async-start(), calls=%async_computation.6 | async-start | bytes 1916928 | tf_op jit(solution)/shard_map/reduce_scatter | solution.py:84
  365.8 3.2 copy-start.1
  371.5 82.0 %all-to-all-start = ((bf16[32,4,208,52]{2,1,3,0:T(4,128)(2,1)}), bf16[32,4,208,52]{2,1,3,0:T(4,128)(2,1)S(1)}, u32[]{:S(2)}, u32[]{:S(2)}) async-start(bf16[32,4,208,52]{2,1,3,0:T(4,128)(2,1)} %stack.2), calls=%async_computation.1 | async-start | bytes 6815744 | tf_op jit(solution)/shard_map/all_to_all | solution.py:19
  378.0 53.5 %all-gather.9.cloned.1.call-start = ((), (), s32[]{:S(2)}) async-start(), calls=%async_computation.7 | async-start | bytes 1916928 | tf_op jit(solution)/shard_map/all_gather | solution.py:88
  404.6 86.6 %reduce-scatter.7.cloned.1.call-start = ((), (), s32[]{:S(2)}) async-start(), calls=%async_computation.8 | async-start | bytes 479232
  453.6 2.8 copy-start.3
Sparse Core Ops, SparseCore 0:
  10.6 96.3 all-gather.4
  109.6 88.6 all-gather.6
  369.0 33.7 reduce-scatter.4
  405.2 26.2 all-gather.8
  456.5 34.6 reduce-scatter.6
